TPU v7x, 32 devices: a whole 2x2x4 slice. The times are simulated.
32 devices in a mesh: row: 4 (over z), col: 8 (over y, x, core).
Axes of the slice: x: 2, y: 2, z: 4, core: 2. Of those that a mesh axis runs over, the one named last changes fastest.
Arguments:
- block_cells: float32 [352, 5, 16, 256], P(('row', 'col')), may hold values from -0.6 to 1.4, as said below
- slot_blocks: int32 [32, 11], replicated, may hold values from -1 to 191, as said below
Outputs:
- new_cells: float32 [224, 5, 16, 256], P(('row', 'col'))
Inputs may be any that keep to these rules, and one draw needn't show every extreme that they name: `slot_blocks`: row r * 8 + c lists the blocks held by device (r, c): block ids first, in slot order, then -1. Block b belongs to column group b // 24, and every block of column group c is held by exactly one device of that column group. Each device holds 1 to 11 blocks, the devices of a column group hold 24 blocks together, and in every column group one device holds 11 blocks and one holds 1. `block_cells`: fields 0 and 4 (density, pressure) lie in 0.7 to 1.4 and fields 1 to 3 (velocity) in -0.6 to 0.6. Slots marked -1 in slot_blocks hold values that no output depends on.
All inputs are finite; a program needn't handle non-finite values.
Results may differ from a plain program's by a relative error of at most 0.0001.
Values sent between devices are 32-bit elements; how exact they have to be, the bound alone decides.
A program may use at most 64 MiB of HBM per device.

v0:
```python
import jax
import jax.numpy as jnp
from jax import lax
from jax.sharding import PartitionSpec as P

BLK_MEAN = 6
OUT = 7


heat_ratio = 1.4
time_step = 0.12
thermal_leading_multiplier = 0.2
thermal_power_law_index = 0.7


def swapped(array, axis, apart):
    return lax.ppermute(array, axis, [(i, i ^ 1 << apart) for i in range(lax.axis_size(axis))])


def from_behind(block, axis, distance):
    devices = range(lax.axis_size(axis))
    route = [((i - distance) % len(devices), i) for i in devices]
    return lax.ppermute(block, axis, route)


def rebalance_table(anchors, counts):
    row_count, columns, slot_width = anchors.shape
    slot_ids = jnp.arange(slot_width, dtype=jnp.int32)
    row_ids = jnp.arange(row_count, dtype=jnp.int32)
    for section_bit in range(row_count.bit_length() - 1):
        partner = row_ids ^ 1 << section_bit
        other_anchors = anchors[partner]
        other_counts = counts[partner]
        sending = jnp.maximum(counts - other_counts, 0) // 2
        taking = jnp.maximum(other_counts - counts, 0) // 2
        keeping = (counts - sending)[:, :, None]
        anchor_slot = other_counts[:, :, None] - taking[:, :, None] + slot_ids - keeping
        pulled = jnp.take_along_axis(
            other_anchors, jnp.clip(anchor_slot, 0, slot_width - 1), axis=2
        )
        anchors = jnp.where(
            slot_ids < keeping,
            anchors,
            jnp.where(slot_ids < keeping + taking[:, :, None], pulled, -1),
        )
        counts = counts - sending + taking
    return (anchors, counts)


def to_conserved(primitive):
    matter_per_volume = primitive[0]
    velocity = primitive[1:4]
    fluid_static_stress = primitive[4]
    energy = fluid_static_stress / (heat_ratio - 1.0) + 0.5 * matter_per_volume * jnp.sum(
        velocity * velocity, axis=0
    )
    return jnp.concatenate(
        [matter_per_volume[None], matter_per_volume[None] * velocity, energy[None]], axis=0
    )


def to_primitive(conserved):
    matter_per_volume = conserved[0]
    velocity = conserved[1:4] / matter_per_volume
    fluid_static_stress = (heat_ratio - 1.0) * (
        conserved[4] - 0.5 * matter_per_volume * jnp.sum(velocity * velocity, axis=0)
    )
    return jnp.concatenate([matter_per_volume[None], velocity, fluid_static_stress[None]], axis=0)


def cell_terms(conserved, normal):
    matter_per_volume = conserved[0]
    momentum = conserved[1:4]
    velocity = momentum / matter_per_volume
    fluid_static_stress = (heat_ratio - 1.0) * (
        conserved[4] - 0.5 * matter_per_volume * jnp.sum(velocity * velocity, axis=0)
    )
    perpendicular_flow_rate = velocity[normal]
    moment_flux = momentum * perpendicular_flow_rate
    moment_flux = moment_flux.at[normal].add(fluid_static_stress)
    face_transport_amounts = jnp.concatenate(
        [
            momentum[normal][None],
            moment_flux,
            ((conserved[4] + fluid_static_stress) * perpendicular_flow_rate)[None],
        ],
        axis=0,
    )
    sound_signal_rate = jnp.sqrt(heat_ratio * fluid_static_stress / matter_per_volume)
    fluid_thermal_state = fluid_static_stress / matter_per_volume
    thermal_diffusivity_factor = thermal_leading_multiplier * jnp.power(
        fluid_thermal_state, thermal_power_law_index
    )
    return (
        face_transport_amounts,
        jnp.abs(perpendicular_flow_rate) + sound_signal_rate,
        fluid_thermal_state,
        thermal_diffusivity_factor,
        fluid_static_stress,
    )


def face_flux(lower_cons, lower_data, upper_cons, upper_data):
    wave_speed = jnp.maximum(lower_data[1], upper_data[1])
    face_transport_amounts = 0.5 * (lower_data[0] + upper_data[0]) - 0.5 * wave_speed[None] * (
        upper_cons - lower_cons
    )
    heat_flow = 0.5 * (lower_data[3] + upper_data[3]) * (upper_data[2] - lower_data[2])
    return face_transport_amounts.at[4].add(-heat_flow)


def wall_flux(fluid_static_stress, normal):
    nothing = jnp.zeros_like(fluid_static_stress)
    members = [nothing, nothing, nothing, nothing, nothing]
    members[normal + 1] = fluid_static_stress
    return jnp.stack(members, axis=0)


def cut_rows(tree, first_index, last_index):
    return jax.tree.map(lambda member: member[..., first_index:last_index, :], tree)


def cut_flat(tree, first_index, last_index):
    return jax.tree.map(lambda member: member[..., first_index:last_index], tree)


def block_tendency(conserved, low_x, high_x, low_y, high_y):
    block_edge = conserved.shape[1]
    flat_size = conserved.shape[2]
    padded_x = jnp.concatenate([low_x, conserved, high_x], axis=1)
    cell_data = cell_terms(padded_x, 0)
    face_transport_amounts = face_flux(
        padded_x[:, :-1],
        cut_rows(cell_data, 0, block_edge + 1),
        padded_x[:, 1:],
        cut_rows(cell_data, 1, block_edge + 2),
    )
    change_x = face_transport_amounts[:, 1:] - face_transport_amounts[:, :-1]
    padded_y = jnp.concatenate([low_y, conserved, high_y], axis=2)
    cell_data = cell_terms(padded_y, 1)
    reach_end = flat_size + block_edge
    face_transport_amounts = face_flux(
        padded_y[..., :reach_end],
        cut_flat(cell_data, 0, reach_end),
        padded_y[..., block_edge:],
        cut_flat(cell_data, block_edge, reach_end + block_edge),
    )
    change_y = face_transport_amounts[..., block_edge:] - face_transport_amounts[..., :flat_size]
    cell_data = cell_terms(conserved, 2)
    interior = face_flux(
        conserved[..., :-1],
        cut_flat(cell_data, 0, flat_size - 1),
        conserved[..., 1:],
        cut_flat(cell_data, 1, flat_size),
    )
    nothing = jnp.zeros_like(interior[..., :1])
    wall_values = wall_flux(cell_data[4], 2)
    height = jnp.arange(flat_size, dtype=jnp.int32) % block_edge
    upper_face = jnp.where(
        height == block_edge - 1, wall_values, jnp.concatenate([interior, nothing], axis=-1)
    )
    lower_face = jnp.where(height == 0, wall_values, jnp.concatenate([nothing, interior], axis=-1))
    change_z = upper_face - lower_face
    return -(change_x + change_y + change_z)


def body(block_cells, slot_blocks):
    row_count = lax.axis_size("row")
    columns = lax.axis_size("col")
    my_row = lax.axis_index("row")
    my_col = lax.axis_index("col")
    slot_width = slot_blocks.shape[1]
    per_group = BLK_MEAN * row_count
    send_slots = BLK_MEAN - 1
    block_edge = block_cells.shape[2]
    flat_size = block_cells.shape[3]
    every_slot = slot_blocks.reshape(-1)
    occupied = slot_blocks >= 0
    counts = jnp.sum(occupied.astype(jnp.int32), axis=1).reshape(row_count, columns)
    device_ids = jnp.arange(row_count * columns, dtype=jnp.int32)[:, None]
    anchors = jnp.where(
        occupied, device_ids * slot_width + jnp.arange(slot_width, dtype=jnp.int32)[None, :], -1
    )
    anchors = anchors.reshape(row_count, columns, slot_width)
    final_anchors, final_counts = rebalance_table(anchors, counts)
    final_anchors = final_anchors[:, :, :OUT]
    my_anchors = final_anchors[my_row, my_col]
    row_ids = jnp.arange(row_count, dtype=jnp.int32)
    holding = block_cells
    counts_now = counts
    slot_ids = jnp.arange(slot_width, dtype=jnp.int32)
    for section_bit in range(row_count.bit_length() - 1):
        partner = row_ids ^ 1 << section_bit
        other_counts = counts_now[partner]
        sending = jnp.maximum(counts_now - other_counts, 0) // 2
        taking = jnp.maximum(other_counts - counts_now, 0) // 2
        keeping = counts_now[my_row, my_col] - sending[my_row, my_col]
        send_from = jnp.clip(keeping + jnp.arange(send_slots, dtype=jnp.int32), 0, slot_width - 1)
        outgoing = jnp.take(holding, send_from, axis=0)
        incoming = swapped(outgoing, "row", section_bit)
        candidates = jnp.concatenate([holding, incoming], axis=0)
        chosen = jnp.where(
            slot_ids < keeping,
            slot_ids,
            slot_width + jnp.clip(slot_ids - keeping, 0, send_slots - 1),
        )
        holding = jnp.take(candidates, chosen, axis=0)
        counts_now = counts_now - sending + taking
    holding = holding[:OUT]
    active = my_anchors >= 0
    benign = jnp.array([1.0, 0.0, 0.0, 0.0, 1.0], jnp.float32)[None, :, None, None]
    holding = jnp.where(active[:, None, None, None], holding, benign)
    initial = jax.vmap(to_conserved)(holding)
    my_blocks = every_slot[jnp.maximum(my_anchors, 0)]
    along_y = jnp.clip(my_blocks - my_col * per_group, 0, per_group - 1)
    below_col = (my_col - 1) % columns
    above_col = (my_col + 1) % columns

    def located(column, wanted):
        anchors_here = final_anchors[:, column].reshape(-1)
        blocks_here = jnp.where(anchors_here >= 0, every_slot[jnp.maximum(anchors_here, 0)], -1)
        return jnp.argmax(blocks_here[None, :] == wanted[:, None], axis=1)

    from_x_low = located(below_col, below_col * per_group + along_y)
    from_y_low = located(below_col, below_col * per_group + (along_y - 1) % per_group)
    from_x_high = located(above_col, above_col * per_group + along_y)
    from_y_high = located(above_col, above_col * per_group + (along_y + 1) % per_group)

    def section_rate(current):
        highs = jnp.stack(
            [
                current[:, :, block_edge - 1, :],
                current[:, :, :, flat_size - block_edge :].reshape(OUT, 5, flat_size),
            ],
            axis=1,
        )
        lows = jnp.stack(
            [current[:, :, 0, :], current[:, :, :, :block_edge].reshape(OUT, 5, flat_size)], axis=1
        )
        passed_highs = from_behind(highs, "col", 1)
        passed_lows = from_behind(lows, "col", -1)
        from_below, from_above = (
            lax.all_gather(passed_highs, "row", axis=0, tiled=True),
            lax.all_gather(passed_lows, "row", axis=0, tiled=True),
        )
        low_x = from_below[from_x_low, 0][:, :, None, :]
        low_y = from_below[from_y_low, 1].reshape(OUT, 5, block_edge, block_edge)
        high_x = from_above[from_x_high, 0][:, :, None, :]
        high_y = from_above[from_y_high, 1].reshape(OUT, 5, block_edge, block_edge)
        return jax.vmap(block_tendency)(current, low_x, high_x, low_y, high_y)

    first_section = initial + time_step * section_rate(initial)
    second_section = 0.75 * initial + 0.25 * (
        first_section + time_step * section_rate(first_section)
    )
    third_section = 1.0 / 3.0 * initial + 2.0 / 3.0 * (
        second_section + time_step * section_rate(second_section)
    )
    result = jax.vmap(to_primitive)(third_section)
    return jnp.where(active[:, None, None, None], result, jnp.zeros_like(result)).astype(
        jnp.float32
    )


def solution(mesh):
    in_specs = (P(("row", "col"), None, None, None), P())
    out_specs = P(("row", "col"), None, None, None)
    return jax.shard_map(body, mesh=mesh, in_specs=in_specs, out_specs=out_specs, check_vma=False)
```

profile of v0, /device:TPU:0, one launch (start us, length us, event | category | flops | bytes accessed | tf_op | source)
XLA Modules:
  0.0 179.7 jit_solution(13251556273873494992)
XLA Ops:
  0.0 0.8 copy.142
  1.7 0.6 dynamic_slice.24
  2.3 0.7 dynamic_slice.26
  7.2 1.7 gather_fusion.21
  9.0 3.1 %collective-permute-start = (f32[5,5,16,256]{3,2,1,0:T(8,128)S(1)}, f32[5,5,16,256]{3,2,1,0:T(8,128)S(1)}, u32[]{:S(2)}, u32[]{:S(2)}) collective-permute-start(f32[5,5,16,256]{3,2,1,0:T(8,128)S(1)} %broadcast_select_fusion.2), channel_id=1, source_target_pairs={{0,8},{8,0},{16,24},{24,16},{1,9},{9,1},{17,25},{25,17},{2,10},{10... | collective-permute-start | bytes 1228808 | tf_op jit(solution)/shard_map/ppermute | solution.py:17
  13.4 4.0 %gather_fusion.19 = s32[352]{0:T(512)S(1)} fusion(s32[4,8,11]{2,1,0:T(8,128)S(1)} %gather_fusion.2, s32[352]{0:T(512)S(1)} %reshape.1164), kind=kCustom, calls=%fused_computation.clone | custom fusion | bytes 7040 | tf_op jit(solution)/shard_map/jit(take_along_axis)/gather | solution.py:38
  18.2 4.0 %gather_fusion.20 = s32[352]{0:T(512)S(1)} fusion(s32[4,8,11]{2,1,0:T(8,128)S(1)} %gather_fusion.3, s32[352]{0:T(512)S(1)} %reshape.1169), kind=kCustom, calls=%fused_computation.3.clone | custom fusion | bytes 7040 | tf_op jit(solution)/shard_map/jit(take_along_axis)/gather | solution.py:38
  22.9 0.7 gather_fusion.7
  23.6 0.7 gather_fusion.4
  24.3 0.6 gather_fusion.5
  25.0 0.7 iota_reduce_fusion.2
  25.7 0.7 iota_reduce_fusion
  26.5 0.7 iota_reduce_fusion.3
  27.2 0.7 iota_reduce_fusion.1
  28.0 0.6 gather_fusion.22
  29.5 2.7 %collective-permute-start.1 = (f32[5,5,16,256]{3,2,1,0:T(8,128)S(1)}, f32[5,5,16,256]{3,2,1,0:T(8,128)S(1)}, u32[]{:S(2)}, u32[]{:S(2)}) collective-permute-start(f32[5,5,16,256]{3,2,1,0:T(8,128)S(1)} %broadcast_select_fusion.1), channel_id=1, source_target_pairs={{0,16},{8,24},{16,0},{24,8},{1,17},{9,25},{17,1},{25,9},{2,18},{10... | collective-permute-start | bytes 1228808 | tf_op jit(solution)/shard_map/ppermute | solution.py:17
  32.1 17.8 %collective-permute-done.1 = f32[5,5,16,256]{3,2,1,0:T(8,128)S(1)} collective-permute-done((f32[5,5,16,256]{3,2,1,0:T(8,128)S(1)}, f32[5,5,16,256]{3,2,1,0:T(8,128)S(1)}, u32[]{:S(2)}, u32[]{:S(2)}) %collective-permute-start.1) | collective-permute-done | bytes 409632 | tf_op jit(solution)/shard_map/ppermute | solution.py:17
  50.1 0.6 gather_fusion.24
  52.2 2.2 %collective-permute-start.3 = (f32[7,2,5,256]{3,1,2,0:T(2,128)S(1)}, f32[7,2,5,256]{3,1,2,0:T(2,128)S(1)}, u32[]{:S(2)}, u32[]{:S(2)}) collective-permute-start(f32[7,2,5,256]{3,1,2,0:T(2,128)S(1)} %pad_maximum_fusion.29), channel_id=1, source_target_pairs={{1,0},{2,1},{3,2},{4,3},{5,4},{6,5},{7,6},{0,7},{9,8},{10,9},{11,1... | collective-permute-start | bytes 215048 | tf_op jit(solution)/shard_map/ppermute | solution.py:23
  55.1 4.1 %collective-permute-done.2 = f32[7,2,5,256]{3,1,2,0:T(2,128)S(1)} collective-permute-done((f32[7,2,5,256]{3,1,2,0:T(2,128)S(1)}, f32[7,2,5,256]{3,1,2,0:T(2,128)S(1)}, u32[]{:S(2)}, u32[]{:S(2)}) %collective-permute-start.2) | collective-permute-done | bytes 71712 | tf_op jit(solution)/shard_map/ppermute | solution.py:23
  59.2 14.6 %all_gather.18 = f32[28,2,5,256]{3,1,2,0:T(2,128)S(1)} all-gather(f32[7,2,5,256]{3,1,2,0:T(2,128)S(1)} %collective-permute-done.2), channel_id=1, replica_groups=mesh['row'=4,'col'=8] {'row'}, dimensions={0}, use_global_device_ids=true | all-gather | bytes 358400 | tf_op jit(solution)/shard_map/all_gather | solution.py:243
  74.4 13.9 %all_gather.19 = f32[28,2,5,256]{3,1,2,0:T(2,128)S(1)} all-gather(f32[7,2,5,256]{3,1,2,0:T(2,128)S(1)} %collective-permute-done.3), channel_id=1, replica_groups=mesh['row'=4,'col'=8] {'row'}, dimensions={0}, use_global_device_ids=true | all-gather | bytes 358400 | tf_op jit(solution)/shard_map/all_gather | solution.py:244
  90.4 1.6 gather_fusion.8
  96.8 0.7 collective-permute-start.4
  98.1 3.6 %collective-permute-done.4 = f32[7,2,5,256]{3,1,2,0:T(2,128)S(1)} collective-permute-done((f32[7,2,5,256]{3,1,2,0:T(2,128)S(1)}, f32[7,2,5,256]{3,1,2,0:T(2,128)S(1)}, u32[]{:S(2)}, u32[]{:S(2)}) %collective-permute-start.4) | collective-permute-done | bytes 71712 | tf_op jit(solution)/shard_map/ppermute | solution.py:23
  101.7 14.2 %all_gather.20 = f32[28,2,5,256]{3,1,2,0:T(2,128)S(1)} all-gather(f32[7,2,5,256]{3,1,2,0:T(2,128)S(1)} %collective-permute-done.4), channel_id=1, replica_groups=mesh['row'=4,'col'=8] {'row'}, dimensions={0}, use_global_device_ids=true | all-gather | bytes 358400 | tf_op jit(solution)/shard_map/all_gather | solution.py:243
  117.1 14.4 %all_gather.21 = f32[28,2,5,256]{3,1,2,0:T(2,128)S(1)} all-gather(f32[7,2,5,256]{3,1,2,0:T(2,128)S(1)} %collective-permute-done.5), channel_id=1, replica_groups=mesh['row'=4,'col'=8] {'row'}, dimensions={0}, use_global_device_ids=true | all-gather | bytes 358400 | tf_op jit(solution)/shard_map/all_gather | solution.py:244
  139.6 3.6 %collective-permute-done.6 = f32[7,2,5,256]{3,1,2,0:T(2,128)S(1)} collective-permute-done((f32[7,2,5,256]{3,1,2,0:T(2,128)S(1)}, f32[7,2,5,256]{3,1,2,0:T(2,128)S(1)}, u32[]{:S(2)}, u32[]{:S(2)}) %collective-permute-start.6) | collective-permute-done | bytes 71712 | tf_op jit(solution)/shard_map/ppermute | solution.py:23
  143.2 14.1 %all_gather.22 = f32[28,2,5,256]{3,1,2,0:T(2,128)S(1)} all-gather(f32[7,2,5,256]{3,1,2,0:T(2,128)S(1)} %collective-permute-done.6), channel_id=1, replica_groups=mesh['row'=4,'col'=8] {'row'}, dimensions={0}, use_global_device_ids=true | all-gather | bytes 358400 | tf_op jit(solution)/shard_map/all_gather | solution.py:243
  158.6 14.4 %all_gather.23 = f32[28,2,5,256]{3,1,2,0:T(2,128)S(1)} all-gather(f32[7,2,5,256]{3,1,2,0:T(2,128)S(1)} %collective-permute-done.7), channel_id=1, replica_groups=mesh['row'=4,'col'=8] {'row'}, dimensions={0}, use_global_device_ids=true | all-gather | bytes 358400 | tf_op jit(solution)/shard_map/all_gather | solution.py:244
  178.0 0.6 fusion.47
  178.9 0.8 copy.184
  (257 shorter events, 31.5 us)
Async XLA Ops:
  9.0 18.9 %collective-permute-start = (f32[5,5,16,256]{3,2,1,0:T(8,128)S(1)}, f32[5,5,16,256]{3,2,1,0:T(8,128)S(1)}, u32[]{:S(2)}, u32[]{:S(2)}) collective-permute-start(f32[5,5,16,256]{3,2,1,0:T(8,128)S(1)} %broadcast_select_fusion.2), channel_id=1, source_target_pairs={{0,8},{8,0},{16,24},{24,16},{1,9},{9,1},{17,25},{25,17},{2,10},{10... | collective-permute-start | bytes 1228808 | tf_op jit(solution)/shard_map/ppermute | solution.py:17
  22.2 5.7 %copy-start = (f32[11,5,16,256]{3,2,1,0:T(8,128)S(1)}, f32[11,5,16,256]{3,2,1,0:T(8,128)}, u32[]{:S(2)}) copy-start(f32[11,5,16,256]{3,2,1,0:T(8,128)} %param.45) | copy-start | bytes 2703364
  29.5 20.5 %collective-permute-start.1 = (f32[5,5,16,256]{3,2,1,0:T(8,128)S(1)}, f32[5,5,16,256]{3,2,1,0:T(8,128)S(1)}, u32[]{:S(2)}, u32[]{:S(2)}) collective-permute-start(f32[5,5,16,256]{3,2,1,0:T(8,128)S(1)} %broadcast_select_fusion.1), channel_id=1, source_target_pairs={{0,16},{8,24},{16,0},{24,8},{1,17},{9,25},{17,1},{25,9},{2,18},{10... | collective-permute-start | bytes 1228808 | tf_op jit(solution)/shard_map/ppermute | solution.py:17
  50.1 0.7 copy-start.2
  52.2 22.2 %collective-permute-start.3 = (f32[7,2,5,256]{3,1,2,0:T(2,128)S(1)}, f32[7,2,5,256]{3,1,2,0:T(2,128)S(1)}, u32[]{:S(2)}, u32[]{:S(2)}) collective-permute-start(f32[7,2,5,256]{3,1,2,0:T(2,128)S(1)} %pad_maximum_fusion.29), channel_id=1, source_target_pairs={{1,0},{2,1},{3,2},{4,3},{5,4},{6,5},{7,6},{0,7},{9,8},{10,9},{11,1... | collective-permute-start | bytes 215048 | tf_op jit(solution)/shard_map/ppermute | solution.py:23
  54.5 4.7 %collective-permute-start.2 = (f32[7,2,5,256]{3,1,2,0:T(2,128)S(1)}, f32[7,2,5,256]{3,1,2,0:T(2,128)S(1)}, u32[]{:S(2)}, u32[]{:S(2)}) collective-permute-start(f32[7,2,5,256]{3,1,2,0:T(2,128)S(1)} %pad_maximum_fusion.28), channel_id=1, source_target_pairs={{7,0},{0,1},{1,2},{2,3},{3,4},{4,5},{5,6},{6,7},{15,8},{8,9},{9,10... | collective-permute-start | bytes 215048 | tf_op jit(solution)/shard_map/ppermute | solution.py:23
  88.4 0.8 copy-start.1
  96.6 20.5 %collective-permute-start.5 = (f32[7,2,5,256]{3,1,2,0:T(2,128)S(1)}, f32[7,2,5,256]{3,1,2,0:T(2,128)S(1)}, u32[]{:S(2)}, u32[]{:S(2)}) collective-permute-start(f32[7,2,5,256]{3,1,2,0:T(2,128)S(1)} %pad_maximum_fusion.31), channel_id=1, source_target_pairs={{1,0},{2,1},{3,2},{4,3},{5,4},{6,5},{7,6},{0,7},{9,8},{10,9},{11,1... | collective-permute-start | bytes 215048 | tf_op jit(solution)/shard_map/ppermute | solution.py:23
  96.8 4.9 %collective-permute-start.4 = (f32[7,2,5,256]{3,1,2,0:T(2,128)S(1)}, f32[7,2,5,256]{3,1,2,0:T(2,128)S(1)}, u32[]{:S(2)}, u32[]{:S(2)}) collective-permute-start(f32[7,2,5,256]{3,1,2,0:T(2,128)S(1)} %pad_maximum_fusion.30), channel_id=1, source_target_pairs={{7,0},{0,1},{1,2},{2,3},{3,4},{4,5},{5,6},{6,7},{15,8},{8,9},{9,10... | collective-permute-start | bytes 215048 | tf_op jit(solution)/shard_map/ppermute | solution.py:23
  138.3 20.2 %collective-permute-start.7 = (f32[7,2,5,256]{3,1,2,0:T(2,128)S(1)}, f32[7,2,5,256]{3,1,2,0:T(2,128)S(1)}, u32[]{:S(2)}, u32[]{:S(2)}) collective-permute-start(f32[7,2,5,256]{3,1,2,0:T(2,128)S(1)} %pad_maximum_fusion.33), channel_id=1, source_target_pairs={{1,0},{2,1},{3,2},{4,3},{5,4},{6,5},{7,6},{0,7},{9,8},{10,9},{11,1... | collective-permute-start | bytes 215048 | tf_op jit(solution)/shard_map/ppermute | solution.py:23
  138.5 4.7 %collective-permute-start.6 = (f32[7,2,5,256]{3,1,2,0:T(2,128)S(1)}, f32[7,2,5,256]{3,1,2,0:T(2,128)S(1)}, u32[]{:S(2)}, u32[]{:S(2)}) collective-permute-start(f32[7,2,5,256]{3,1,2,0:T(2,128)S(1)} %pad_maximum_fusion.32), channel_id=1, source_target_pairs={{7,0},{0,1},{1,2},{2,3},{3,4},{4,5},{5,6},{6,7},{15,8},{8,9},{9,10... | collective-permute-start | bytes 215048 | tf_op jit(solution)/shard_map/ppermute | solution.py:23
where the time goes:
time: 180 us
  blocking collectives  85.5 us (48%)
  local copies, waits for them, and re-layouts  32.5 us (18%)
  waiting for transfers between devices  29.1 us (16%)
  other arithmetic  19.2 us (11%)
  starting transfers between devices  9.39 us (5%)
  between operations  3.94 us (2%)
    all_gather x3, blocking collectives, section_rate(): lax.all_gather(passed_highs, 'row', axis=0, tiled=True)  42.9 us
    all_gather x3, blocking collectives, section_rate(): lax.all_gather(passed_lows, 'row', axis=0, tiled=True)  42.7 us
    ppermute x2, waiting for transfers between devices, swapped(): lax.ppermute(array, axis, [(i, i ^ 1 << apart) for i in range(lax.axis_si...  17.8 us
    ppermute x6, waiting for transfers between devices, from_behind(): return lax.ppermute(block, axis, route)  11.3 us
    gather x6, local copies, waits for them, and re-layouts, rebalance_table(): jnp.take_along_axis(other_anchors, jnp.clip(anchor_slot, 0, slot_width -...  8.44 us
    ppermute x2, starting transfers between devices, swapped(): lax.ppermute(array, axis, [(i, i ^ 1 << apart) for i in range(lax.axis_si...  5.78 us
    sub x9, other arithmetic, face_flux(): 0.5 * (lower_data[0] + upper_data[0])  3.63 us
    ppermute x6, starting transfers between devices, from_behind(): return lax.ppermute(block, axis, route)  3.61 us
  transfers between devices with their start and end apart: 8, of which 4 were waited for; matrix products, arithmetic and copies ran while one was open for 11% of the time, Pallas kernels for 0%

commit v1 on v0

v1 whole, which is shorter than its diff:
```python
import functools

import jax
import jax.numpy as jnp
from jax import lax
from jax.experimental import pallas as pl
from jax.experimental.pallas import tpu as pltpu
from jax.sharding import PartitionSpec as P

MESH = pl.DeviceIdType.MESH
BLK_MEAN = 6
OUT = 7
SEND = BLK_MEAN - 1
LANES = 128
DT = 0.12


def make_tables(slot_blocks, rows, cols, my_row, my_col):
    cap = slot_blocks.shape[1]
    levels = rows.bit_length() - 1
    half = rows // 2
    group = BLK_MEAN * rows
    ids = slot_blocks.reshape(rows, cols, cap)
    counts = jnp.sum((ids >= 0).astype(jnp.int32), axis=2)
    row_ids = jnp.arange(rows, dtype=jnp.int32)
    col_ids = jnp.arange(cols, dtype=jnp.int32)
    at_row = jnp.broadcast_to(row_ids[:, None, None], ids.shape)
    at_slot = jnp.broadcast_to(jnp.arange(cap, dtype=jnp.int32), ids.shape)
    mine = (row_ids[:, None] == my_row) & (col_ids[None, :] == my_col)
    scalars = []
    for level in range(levels):
        bit = 1 << level
        other = counts.reshape(rows // (2 * bit), 2, bit, cols)[:, ::-1].reshape(rows, cols)
        send = jnp.maximum(counts - other, 0) // 2
        take = jnp.maximum(other - counts, 0) // 2
        keep = counts - send
        scalars.append(jnp.sum(jnp.where(mine, keep, 0)))
        hit = at_row[None] == row_ids[:, None, None, None]
        keep_here = jnp.sum(jnp.where(hit, keep[:, None, :, None], 0), axis=0)
        other_here = jnp.sum(jnp.where(hit, other[:, None, :, None], 0), axis=0)
        moved = at_slot >= keep_here
        at_row = jnp.where(moved, at_row ^ bit, at_row)
        at_slot = jnp.where(moved, other_here + at_slot - keep_here, at_slot)
        counts = keep + take
    scalars.append(jnp.sum(jnp.where(mine, counts, 0)))
    place = at_row * 8 + at_slot
    flat_ids = ids.reshape(-1)
    flat_place = jnp.where(flat_ids >= 0, place.reshape(-1), 0)
    flat_col = jnp.broadcast_to(col_ids[None, :, None], ids.shape).reshape(-1)
    seats = jnp.stack([my_row, my_row ^ half])[:, None] * 8 + jnp.arange(OUT, dtype=jnp.int32)
    seats = seats.reshape(-1)
    match = (flat_place[None] == seats[:, None]) & (flat_col == my_col)[None] & (flat_ids >= 0)[None]
    along = jnp.sum(jnp.where(match, flat_ids[None] - my_col * group, 0), axis=1)
    below = ((my_col + cols - 1) % cols) * group
    above = ((my_col + 1) % cols) * group
    wanted = jnp.stack(
        [
            below + along,
            below + (along + group - 1) % group,
            above + along,
            above + (along + 1) % group,
        ]
    ).reshape(-1)
    found = jnp.sum(jnp.where(flat_ids[None] == wanted[:, None], flat_place[None], 0), axis=1)
    distance = (found // 8) ^ my_row
    source = distance * 8 + found % 8
    return jnp.concatenate([jnp.stack(scalars), source])


def cell_values(cons):
    rho, mx, my, mz, energy = cons
    inv = 1.0 / rho
    vel = (mx * inv, my * inv, mz * inv)
    p = 0.4 * (energy - 0.5 * rho * (vel[0] * vel[0] + vel[1] * vel[1] + vel[2] * vel[2]))
    theta = p * inv
    sound = jnp.sqrt(1.4 * theta)
    kappa = 0.2 * jnp.exp(0.7 * jnp.log(theta))
    return vel, p, theta, sound, kappa


def direction_values(cons, values, normal):
    vel, p, theta, sound, kappa = values
    un = vel[normal]
    flux = [cons[1 + normal], cons[1] * un, cons[2] * un, cons[3] * un, (cons[4] + p) * un]
    flux[1 + normal] = flux[1 + normal] + p
    return (*cons, *flux, jnp.abs(un) + sound, theta, kappa)


def face(low, high):
    half_speed = 0.5 * jnp.maximum(low[10], high[10])
    out = [0.5 * (low[5 + i] + high[5 + i]) - half_speed * (high[i] - low[i]) for i in range(5)]
    out[4] = out[4] - 0.5 * (low[12] + high[12]) * (high[11] - low[11])
    return out


def block_rate(cons, ghost_x, ghost_y):
    edge, flat = cons[0].shape
    row = lax.broadcasted_iota(jnp.int32, (edge, flat), 0)
    lane = lax.broadcasted_iota(jnp.int32, (edge, flat), 1)
    values = cell_values(cons)
    mid = direction_values(cons, values, 0)
    gx = direction_values(ghost_x, cell_values(ghost_x), 0)
    last = row == edge - 1
    up = [
        jnp.where(last, jnp.concatenate([g, g], axis=0), pltpu.roll(m, edge - 1, 0))
        for m, g in zip(mid, gx)
    ]
    upper = face(mid, up)
    bottom = face(gx, [m[:8] for m in mid])
    change = [
        u - jnp.where(row == 0, jnp.concatenate([b, b], axis=0), pltpu.roll(u, 1, 0))
        for u, b in zip(upper, bottom)
    ]
    mid = direction_values(cons, values, 1)
    gy = direction_values(ghost_y, cell_values(ghost_y), 1)
    last = lane >= flat - edge
    up = [
        jnp.where(last, jnp.concatenate([g, g], axis=1), pltpu.roll(m, flat - edge, 1))
        for m, g in zip(mid, gy)
    ]
    upper = face(mid, up)
    bottom = face(gy, [m[:, :LANES] for m in mid])
    change = [
        t + (u - jnp.where(lane < edge, jnp.concatenate([b, b], axis=1), pltpu.roll(u, edge, 1)))
        for t, u, b in zip(change, upper, bottom)
    ]
    mid = direction_values(cons, values, 2)
    up = [pltpu.roll(m, flat - 1, 1) for m in mid]
    upper = face(mid, up)
    height = lane % edge
    zero = jnp.zeros_like(values[1])
    wall = [zero, zero, zero, values[1], zero]
    change = [
        t
        + (
            jnp.where(height == edge - 1, w, u)
            - jnp.where(height == 0, w, pltpu.roll(u, 1, 1))
        )
        for t, u, w in zip(change, upper, wall)
    ]
    return [-t for t in change]


def kernel(rows, cols, cap, *refs):
    levels = rows.bit_length() - 1
    half = rows // 2
    refs = list(refs)
    tab, cells, out = refs[:3]
    refs = refs[3:]
    send_blocks = refs[:levels]
    recv_blocks = refs[levels : 2 * levels]
    refs = refs[2 * levels :]
    start, now = refs[:2]
    sections = [refs[2 + 8 * i : 10 + 8 * i] for i in range(3)]
    bsend, brecv, hsend, hrecv = refs[26:30]
    my_row, my_col = lax.axis_index("row"), lax.axis_index("col")
    left = (my_row, lax.rem(my_col + cols - 1, cols))
    right = (my_row, lax.rem(my_col + 1, cols))

    def partner(level):
        bit = 1 << level
        return (my_row + bit - 2 * bit * (lax.rem(my_row // bit, 2)), my_col)

    barrier = pltpu.get_barrier_semaphore()
    for device in [left, right] + [partner(level) for level in range(levels)]:
        pl.semaphore_signal(barrier, inc=1, device_id=device, device_id_type=MESH)
    pl.semaphore_wait(barrier, 2 + levels)

    def held(slot, depth):
        value = cells[jnp.minimum(slot, cap - 1)]
        for level in range(depth):
            keep = tab[level]
            got = recv_blocks[level][jnp.clip(slot - keep, 0, SEND - 1)]
            value = jnp.where(slot >= keep, got, value)
        return value

    for level in range(levels):
        for k in range(SEND):
            send_blocks[level][k] = held(tab[level] + k, level)
        copy = pltpu.make_async_remote_copy(
            src_ref=send_blocks[level],
            dst_ref=recv_blocks[level],
            send_sem=bsend.at[level],
            recv_sem=brecv.at[level],
            device_id=partner(level),
            device_id_type=MESH,
        )
        copy.start()
        copy.wait()

    def open_block(slot, carry):
        value = held(slot, levels)
        rho, u, v, w, p = (value[f] for f in range(5))
        energy = p / 0.4 + 0.5 * rho * (u * u + v * v + w * w)
        for f, field in enumerate((rho, rho * u, rho * v, rho * w, energy)):
            start[slot, f] = field
            now[slot, f] = field
        return carry

    lax.fori_loop(0, OUT, open_block, 0)

    edge = now.shape[2]
    tile_lane = lax.broadcasted_iota(jnp.int32, (edge, LANES), 1)
    ghost_row = lax.broadcasted_iota(jnp.int32, (8, 2 * LANES), 0)

    for step in range(3):
        hi_send, lo_send, lo_known, hi_known, lo_pick, hi_pick, lo_sel, hi_sel = sections[step]
        used = [0]

        def remote(src, dst, device):
            at = used[0]
            used[0] += 1
            copy = pltpu.make_async_remote_copy(
                src_ref=src,
                dst_ref=dst,
                send_sem=hsend.at[step, at],
                recv_sem=hrecv.at[step, at],
                device_id=device,
                device_id_type=MESH,
            )
            copy.start()
            return copy

        def pack(buffer, high):
            for f in range(5):
                tile = None
                for s in range(OUT):
                    if high:
                        piece = now[s, f, :, LANES : 2 * LANES]
                        shift = (edge * s + edge) % LANES
                    else:
                        piece = now[s, f, :, 0:LANES]
                        shift = edge * s
                    piece = pltpu.roll(piece, shift, 1) if shift else piece
                    tile = piece if tile is None else jnp.where(tile_lane // edge == s, piece, tile)
                    x = edge - 1 if high else 0
                    buffer[5 + f, s : s + 1, :] = now[s, f, x : x + 1, 0:LANES]
                    buffer[5 + f, 8 + s : 9 + s, :] = now[s, f, x : x + 1, LANES : 2 * LANES]
                buffer[f] = tile

        pack(hi_send, True)
        flights_lo = [remote(hi_send, lo_known.at[0], right)]
        pack(lo_send, False)
        flights_hi = [remote(lo_send, hi_known.at[0], left)]

        base = levels + 1

        def entry(kind, far, slot):
            return tab[base + (kind * 2 + far) * OUT + slot]

        def select(known, pick, first_kind):
            for s in range(OUT):
                code = entry(first_kind, 1, s)
                q, sigma = jnp.minimum(code // 8, half - 1), code % 8
                for f in range(5):
                    pick[5 + f, s : s + 1, :] = known[q, 5 + f, pl.ds(sigma, 1), :]
                    pick[5 + f, 8 + s : 9 + s, :] = known[q, 5 + f, pl.ds(8 + sigma, 1), :]
            shifts = []
            for s in range(OUT):
                code = entry(first_kind + 1, 1, s)
                q, sigma = jnp.minimum(code // 8, half - 1), code % 8
                shifts.append((q, lax.rem(edge * (s + 8 - sigma), LANES)))
            for f in range(5):
                tile = None
                for s, (q, shift) in enumerate(shifts):
                    piece = pltpu.roll(known[q, f], shift, 1)
                    tile = piece if tile is None else jnp.where(tile_lane // edge == s, piece, tile)
                pick[f] = tile

        for level in range(levels - 1):
            size = 1 << level
            for known, flights in ((lo_known, flights_lo), (hi_known, flights_hi)):
                flights[-1].wait()
                flights.append(
                    remote(known.at[pl.ds(0, size)], known.at[pl.ds(size, size)], partner(level))
                )
        for known, flights, pick, sel, kind in (
            (lo_known, flights_lo, lo_pick, lo_sel, 0),
            (hi_known, flights_hi, hi_pick, hi_sel, 2),
        ):
            flights[-1].wait()
            select(known, pick, kind)
            flights.append(remote(pick, sel, partner(levels - 1)))
        flights_lo[-1].wait()
        flights_hi[-1].wait()

        def advance(slot, carry):
            def place(kind):
                code = entry(kind, 0, slot)
                near = code < 8 * half
                q = jnp.minimum(code // 8, half - 1)
                return near, q, jnp.where(near, code % 8, slot)

            def x_row(known, sel, seat, f, top):
                near, q, sigma = seat
                a = known[q, 5 + f, pl.ds(top + sigma, 1), :]
                b = sel[5 + f, pl.ds(top + slot, 1), :]
                return jnp.where(near, a, b)

            def y_tile(known, sel, seat, f, to):
                near, q, sigma = seat
                tile = jnp.where(near, known[q, f], sel[f])
                return pltpu.roll(tile, lax.rem(LANES + to - edge * sigma, LANES), 1)

            x_lo, y_lo, x_hi, y_hi = (place(kind) for kind in range(4))
            ghost_x, ghost_y = [], []
            for f in range(5):
                low = jnp.concatenate(
                    [x_row(lo_known, lo_sel, x_lo, f, 0), x_row(lo_known, lo_sel, x_lo, f, 8)], axis=1
                )
                high = jnp.concatenate(
                    [x_row(hi_known, hi_sel, x_hi, f, 0), x_row(hi_known, hi_sel, x_hi, f, 8)], axis=1
                )
                ghost_x.append(jnp.where(ghost_row == 0, low, high))
                ghost_y.append(
                    jnp.where(
                        tile_lane < edge,
                        y_tile(lo_known, lo_sel, y_lo, f, 0),
                        y_tile(hi_known, hi_sel, y_hi, f, LANES - edge),
                    )
                )
            cons = tuple(now[slot, f] for f in range(5))
            rate = block_rate(cons, tuple(ghost_x), tuple(ghost_y))
            moved = [c + DT * d for c, d in zip(cons, rate)]
            if step == 1:
                moved = [0.75 * start[slot, f] + 0.25 * moved[f] for f in range(5)]
            if step == 2:
                moved = [(1.0 / 3.0) * start[slot, f] + (2.0 / 3.0) * moved[f] for f in range(5)]
                rho = moved[0]
                vel = [m / rho for m in moved[1:4]]
                p = 0.4 * (
                    moved[4] - 0.5 * rho * (vel[0] * vel[0] + vel[1] * vel[1] + vel[2] * vel[2])
                )
                filled = slot < tab[levels]
                for f, field in enumerate((rho, *vel, p)):
                    out[slot, f] = jnp.where(filled, field, 0.0)
            else:
                for f in range(5):
                    now[slot, f] = moved[f]
            return carry

        lax.fori_loop(0, OUT, advance, 0)


def body(rows, cols, block_cells, slot_blocks):
    cap = slot_blocks.shape[1]
    levels = rows.bit_length() - 1
    half = rows // 2
    edge, flat = block_cells.shape[2:]
    table = make_tables(slot_blocks, rows, cols, lax.axis_index("row"), lax.axis_index("col"))
    block = (5, edge, flat)
    faces = (10, 16, LANES)
    scratch = [pltpu.VMEM((SEND, *block), jnp.float32) for _ in range(2 * levels)]
    scratch += [pltpu.VMEM((OUT, *block), jnp.float32) for _ in range(2)]
    for _ in range(3):
        scratch += [pltpu.VMEM(faces, jnp.float32) for _ in range(2)]
        scratch += [pltpu.VMEM((half, *faces), jnp.float32) for _ in range(2)]
        scratch += [pltpu.VMEM(faces, jnp.float32) for _ in range(4)]
    scratch += [pltpu.SemaphoreType.DMA((levels,)) for _ in range(2)]
    scratch += [pltpu.SemaphoreType.DMA((3, 2 * (levels + 1))) for _ in range(2)]
    return pl.pallas_call(
        functools.partial(kernel, rows, cols, cap),
        out_shape=jax.ShapeDtypeStruct((OUT, *block), jnp.float32),
        in_specs=[
            pl.BlockSpec(memory_space=pltpu.SMEM),
            pl.BlockSpec(memory_space=pltpu.VMEM),
        ],
        out_specs=pl.BlockSpec(memory_space=pltpu.VMEM),
        scratch_shapes=scratch,
        compiler_params=pltpu.CompilerParams(
            collective_id=0, has_side_effects=True, vmem_limit_bytes=32 << 20
        ),
    )(table, block_cells)


def solution(mesh):
    rows, cols = mesh.shape["row"], mesh.shape["col"]
    return jax.shard_map(
        functools.partial(body, rows, cols),
        mesh=mesh,
        in_specs=(P(("row", "col"), None, None, None), P()),
        out_specs=P(("row", "col"), None, None, None),
        check_vma=False,
    )
```

time: 180 us -> 93.9 us (0.52)
  Pallas kernels: 0 us -> 85.7 us
  blocking collectives: 85.5 us -> 0 us
  waiting for transfers between devices: 29.1 us -> 0 us
  local copies, waits for them, and re-layouts: 32.5 us -> 4.17 us
  other arithmetic: 19.2 us -> 3.68 us
  starting transfers between devices: 9.39 us -> 0 us
  between operations: 3.94 us -> 0.11 us
    pallas_call x0 -> x1, Pallas kernels: none -> 85.7 us  [body(): pl.pallas_call(functools.partial(kernel, rows, cols, cap), out_shape=jax....]
    all_gather x6 -> x0, blocking collectives: 85.5 us -> none  [the longest x3 42.9 us: section_rate(): lax.all_gather(passed_highs, 'row', axis=0, tiled=True)]
    ppermute x8 -> x0, waiting for transfers between devices: 29.1 us -> none  [the longest x2 17.8 us: swapped(): lax.ppermute(array, axis, [(i, i ^ 1 << apart) for i in range(lax.axis_si...]
    gather x35 -> x0, local copies, waits for them, and re-layouts: 24.4 us -> none  [the longest x6 8.44 us: rebalance_table(): jnp.take_along_axis(other_anchors, jnp.clip(anchor_slot, 0, slot_width -...]
    ppermute x8 -> x0, starting transfers between devices: 9.39 us -> none  [the longest x2 5.78 us: swapped(): lax.ppermute(array, axis, [(i, i ^ 1 << apart) for i in range(lax.axis_si...]
    sub x10 -> x0, other arithmetic: 3.65 us -> none  [the longest x9 3.63 us: face_flux(): 0.5 * (lower_data[0] + upper_data[0])]
    another operation x10 -> x1, other arithmetic: 3.2 us -> 0.01 us  [make_tables(): jnp.stack([below + along, below + (along + group - 1) % group, above + al...]
    mul x32 -> x1, other arithmetic: 2.73 us -> 0.08 us  [make_tables(): jnp.stack([my_row, my_row ^ half])[:, None] * 8]
  transfers between devices with their start and end apart: 8 -> 0, of which waited for: 4 -> 0; matrix products, arithmetic and copies ran while one was open for 11% -> 0% of each run, Pallas kernels for 0% -> 0%
where the time goes in v1:
time: 93.9 us; the launch traced here: 93.7 us
  Pallas kernels  85.7 us (91%)
  local copies, waits for them, and re-layouts  4.17 us (4%)
  other arithmetic  3.68 us (4%)
    pallas_call x1, Pallas kernels, body(): pl.pallas_call(functools.partial(kernel, rows, cols, cap), out_shape=jax....  85.7 us
    unnamed x6, local copies, waits for them, and re-layouts  2.69 us
    concatenate x1, other arithmetic, make_tables(): return jnp.concatenate([jnp.stack(scalars), source])  1.96 us

profile of v1, /device:TPU:0, one launch (start us, length us, event | category | flops | bytes accessed | tf_op | source)
XLA Modules:
  0.0 93.7 jit_solution(4821676368622727924)
XLA Ops:
  0.0 0.0 copy-start.1
  0.0 0.1 add_multiply_fusion
  0.1 0.6 copy-done.1
  0.7 0.1 iota_add_fusion
  0.8 0.1 add.281
  0.9 0.1 reduce_sum.105
  1.0 0.1 reshape.442
  1.1 0.1 reduce_sum.103
  1.2 0.8 fusion
  2.0 0.1 eq.114
  2.1 0.1 select_reduce_fusion.3
  2.2 0.1 reduce_sum.111
  2.3 0.1 select_reduce_fusion.4
  2.4 0.1 reduce_sum.109
  2.5 0.1 iota_select_fusion
  2.5 0.1 select_reduce_fusion.1
  2.6 0.1 reduce_sum.115
  2.7 0.1 reduce_sum.113
  2.9 0.1 broadcast_in_dim.116
  2.9 0.1 broadcast_in_dim.119
  3.0 0.1 copy.4
  3.1 0.1 eq.102
  3.2 0.1 broadcast_in_dim.121
  3.4 0.1 broadcast_in_dim.111
  3.5 0.2 select_reduce_fusion.5
  3.7 0.1 eq.115
  3.8 0.2 select_reduce_fusion
  4.0 2.0 %pad_add_fusion.1.refs_0_ = s32[59]{0:T(128)S(1)} fusion(s32[56]{0:T(128)S(1)} %fusion.19, s32[1]{0:T(128)} %bitcast.5, s32[1]{0:T(128)} %bitcast.4, s32[1]{0:T(128)} %bitcast.1), kind=kLoop, calls=%fused_computation.70 | loop fusion | flops 177 | bytes 472 | tf_op jit(solution)/shard_map/concatenate | solution.py:67
  6.0 0.0 copy-start
  6.0 1.2 %copy-done = f32[11,5,16,256]{3,2,1,0:T(8,128)S(1)} copy-done((f32[11,5,16,256]{3,2,1,0:T(8,128)S(1)}, f32[11,5,16,256]{3,2,1,0:T(8,128)}, u32[]{:S(2)}) %copy-start) | copy-done | bytes 901144
  7.1 85.7 %shard_map.28 = f32[7,5,16,256]{3,2,1,0:T(8,128)S(1)} custom-call(s32[59]{0:T(128)S(1)} %pad_add_fusion.1.refs_0_, f32[11,5,16,256]{3,2,1,0:T(8,128)S(1)} %copy-done), custom_call_target="tpu_custom_call" | custom-call | tf_op jit(solution)/shard_map/pallas_call | solution.py:361
  92.8 0.8 copy.6
  (15 shorter events, 0.2 us)
Async XLA Ops:
  0.0 0.7 copy-start.1
  6.0 1.2 %copy-start = (f32[11,5,16,256]{3,2,1,0:T(8,128)S(1)}, f32[11,5,16,256]{3,2,1,0:T(8,128)}, u32[]{:S(2)}) copy-start(f32[11,5,16,256]{3,2,1,0:T(8,128)} %refs_1_.1) | copy-start | bytes 2703364

commit v2 on v1

--- a/solution.py
+++ b/solution.py
@@ -43,11 +43,13 @@
         at_slot = jnp.where(moved, other_here + at_slot - keep_here, at_slot)
         counts = keep + take
     scalars.append(jnp.sum(jnp.where(mine, counts, 0)))
-    place = at_row * 8 + at_slot
+    place = at_row * 16 + at_slot
+    origin = row_ids[:, None, None] * 16 + jnp.arange(cap, dtype=jnp.int32)
+    origin = jnp.broadcast_to(origin, ids.shape).reshape(-1)
     flat_ids = ids.reshape(-1)
     flat_place = jnp.where(flat_ids >= 0, place.reshape(-1), 0)
     flat_col = jnp.broadcast_to(col_ids[None, :, None], ids.shape).reshape(-1)
-    seats = jnp.stack([my_row, my_row ^ half])[:, None] * 8 + jnp.arange(OUT, dtype=jnp.int32)
+    seats = jnp.stack([my_row, my_row ^ half])[:, None] * 16 + jnp.arange(OUT, dtype=jnp.int32)
     seats = seats.reshape(-1)
     match = (flat_place[None] == seats[:, None]) & (flat_col == my_col)[None] & (flat_ids >= 0)[None]
     along = jnp.sum(jnp.where(match, flat_ids[None] - my_col * group, 0), axis=1)
@@ -61,9 +63,10 @@
             above + (along + 1) % group,
         ]
     ).reshape(-1)
-    found = jnp.sum(jnp.where(flat_ids[None] == wanted[:, None], flat_place[None], 0), axis=1)
-    distance = (found // 8) ^ my_row
-    source = distance * 8 + found % 8
+    both = flat_place * 4096 + origin
+    found = jnp.sum(jnp.where(flat_ids[None] == wanted[:, None], both[None], 0), axis=1)
+    source = found ^ (my_row * 16 * 4097)
+    source = jnp.concatenate([source % 4096, source // 4096])
     return jnp.concatenate([jnp.stack(scalars), source])
 
 
@@ -76,6 +79,12 @@
     sound = jnp.sqrt(1.4 * theta)
     kappa = 0.2 * jnp.exp(0.7 * jnp.log(theta))
     return vel, p, theta, sound, kappa
+
+
+def conserved(primitive):
+    rho, u, v, w, p = primitive
+    energy = p / 0.4 + 0.5 * rho * (u * u + v * v + w * w)
+    return (rho, rho * u, rho * v, rho * w, energy)
 
 
 def direction_values(cons, values, normal):
@@ -141,6 +150,24 @@
     return [-t for t in change]
 
 
+def y_units(n):
+    return 2 * ((5 * n + 7) // 8)
+
+
+def units(n):
+    return y_units(n) + (10 * n + 7) // 8
+
+
+def y_seat(slot, f):
+    at = slot * 5 + f
+    return 2 * (at // 8), 16 * (at % 8)
+
+
+def x_seat(n, slot, f, part):
+    at = slot * 10 + 2 * f + part
+    return y_units(n) + at // 8, at % 8
+
+
 def kernel(rows, cols, cap, *refs):
     levels = rows.bit_length() - 1
     half = rows // 2
@@ -174,7 +201,18 @@
             value = jnp.where(slot >= keep, got, value)
         return value
 
-    for level in range(levels):
+    edge, flat = now.shape[2:]
+    tile_lane = lax.broadcasted_iota(jnp.int32, (edge, LANES), 1)
+    ghost_row = lax.broadcasted_iota(jnp.int32, (8, 2 * LANES), 0)
+
+    def tile_of(ref, *seat):
+        *lead, unit = seat
+        return ref[(*lead, pl.ds(unit, 2))].reshape(edge, LANES)
+
+    def put_tile(ref, unit, tile):
+        ref[unit : unit + 2] = tile.reshape(2, 8, LANES)
+
+    def move_blocks(level):
         for k in range(SEND):
             send_blocks[level][k] = held(tab[level] + k, level)
         copy = pltpu.make_async_remote_copy(
@@ -186,139 +224,140 @@
             device_id_type=MESH,
         )
         copy.start()
-        copy.wait()
+        return copy
+
+    def remote(step, at, src, dst, device):
+        copy = pltpu.make_async_remote_copy(
+            src_ref=src,
+            dst_ref=dst,
+            send_sem=hsend.at[step, at],
+            recv_sem=hrecv.at[step, at],
+            device_id=device,
+            device_id_type=MESH,
+        )
+        copy.start()
+        return copy
+
+    def pack(blocks, n, buffer, high):
+        x = edge - 1 if high else 0
+        side = slice(LANES, 2 * LANES) if high else slice(0, LANES)
+        for first in range(0, 5 * n, 8):
+            tile = None
+            for at in range(first, min(first + 8, 5 * n)):
+                s, f = at // 5, at % 5
+                shift = (edge * (at - first) + (edge if high else 0)) % LANES
+                piece = blocks[s, f, :, side]
+                piece = pltpu.roll(piece, shift, 1) if shift else piece
+                tile = piece if tile is None else jnp.where(tile_lane // edge == at - first, piece, tile)
+            put_tile(buffer, 2 * (first // 8), tile)
+        for s in range(n):
+            for f in range(5):
+                for part in range(2):
+                    unit, row = x_seat(n, s, f, part)
+                    buffer[unit, row : row + 1, :] = blocks[
+                        s, f, x : x + 1, part * LANES : (part + 1) * LANES
+                    ]
+
+    base = levels + 1
+
+    def entry(step, kind, far, slot):
+        return tab[base + ((8 * OUT if step else 0) + (kind * 2 + far) * OUT + slot)]
+
+    def near_seat(code):
+        return jnp.minimum(code // 16, half - 1), code % 16
+
+    def select(step, n, known, pick, first_kind):
+        for s in range(OUT):
+            q, sigma = near_seat(entry(step, first_kind, 1, s))
+            for f in range(5):
+                for part in range(2):
+                    unit, row = x_seat(n, sigma, f, part)
+                    to, at = x_seat(OUT, s, f, part)
+                    pick[to, at : at + 1, :] = known[q, unit, pl.ds(row, 1), :]
+        seats = [near_seat(entry(step, first_kind + 1, 1, s)) for s in range(OUT)]
+        for first in range(0, 5 * OUT, 8):
+            tile = None
+            for at in range(first, min(first + 8, 5 * OUT)):
+                q, sigma = seats[at // 5]
+                unit, lane = y_seat(sigma, at % 5)
+                shift = lax.rem(edge * (at - first) + LANES - lane, LANES)
+                piece = pltpu.roll(tile_of(known, q, unit), shift, 1)
+                tile = piece if tile is None else jnp.where(tile_lane // edge == at - first, piece, tile)
+            put_tile(pick, 2 * (first // 8), tile)
+
+    def begin(step, blocks, n):
+        hi_send, lo_send, lo_known, hi_known = sections[step][:4]
+        pack(blocks, n, hi_send, True)
+        low = remote(step, 0, hi_send, lo_known.at[0], right)
+        pack(blocks, n, lo_send, False)
+        return [low, remote(step, 1, lo_send, hi_known.at[0], left)]
+
+    def gather(step, flights):
+        at = 2
+        for level in range(levels - 1):
+            size = 1 << level
+            for side in range(2):
+                known = sections[step][2 + side]
+                flights[side].wait()
+                flights[side] = remote(
+                    step, at, known.at[pl.ds(0, size)], known.at[pl.ds(size, size)], partner(level)
+                )
+                at += 1
+        return flights
+
+    def trade(step, n, flights):
+        for side in range(2):
+            known, pick, sel = (sections[step][at + side] for at in (2, 4, 6))
+            flights[side].wait()
+            select(step, n, known, pick, 2 * side)
+            flights[side] = remote(step, 2 * levels + side, pick, sel, partner(levels - 1))
+        return flights
 
     def open_block(slot, carry):
         value = held(slot, levels)
-        rho, u, v, w, p = (value[f] for f in range(5))
-        energy = p / 0.4 + 0.5 * rho * (u * u + v * v + w * w)
-        for f, field in enumerate((rho, rho * u, rho * v, rho * w, energy)):
+        for f, field in enumerate(conserved([value[f] for f in range(5)])):
             start[slot, f] = field
             now[slot, f] = field
         return carry
 
-    lax.fori_loop(0, OUT, open_block, 0)
-
-    edge = now.shape[2]
-    tile_lane = lax.broadcasted_iota(jnp.int32, (edge, LANES), 1)
-    ghost_row = lax.broadcasted_iota(jnp.int32, (8, 2 * LANES), 0)
-
-    for step in range(3):
-        hi_send, lo_send, lo_known, hi_known, lo_pick, hi_pick, lo_sel, hi_sel = sections[step]
-        used = [0]
-
-        def remote(src, dst, device):
-            at = used[0]
-            used[0] += 1
-            copy = pltpu.make_async_remote_copy(
-                src_ref=src,
-                dst_ref=dst,
-                send_sem=hsend.at[step, at],
-                recv_sem=hrecv.at[step, at],
-                device_id=device,
-                device_id_type=MESH,
-            )
-            copy.start()
-            return copy
-
-        def pack(buffer, high):
-            for f in range(5):
-                tile = None
-                for s in range(OUT):
-                    if high:
-                        piece = now[s, f, :, LANES : 2 * LANES]
-                        shift = (edge * s + edge) % LANES
-                    else:
-                        piece = now[s, f, :, 0:LANES]
-                        shift = edge * s
-                    piece = pltpu.roll(piece, shift, 1) if shift else piece
-                    tile = piece if tile is None else jnp.where(tile_lane // edge == s, piece, tile)
-                    x = edge - 1 if high else 0
-                    buffer[5 + f, s : s + 1, :] = now[s, f, x : x + 1, 0:LANES]
-                    buffer[5 + f, 8 + s : 9 + s, :] = now[s, f, x : x + 1, LANES : 2 * LANES]
-                buffer[f] = tile
-
-        pack(hi_send, True)
-        flights_lo = [remote(hi_send, lo_known.at[0], right)]
-        pack(lo_send, False)
-        flights_hi = [remote(lo_send, hi_known.at[0], left)]
-
-        base = levels + 1
-
-        def entry(kind, far, slot):
-            return tab[base + (kind * 2 + far) * OUT + slot]
-
-        def select(known, pick, first_kind):
-            for s in range(OUT):
-                code = entry(first_kind, 1, s)
-                q, sigma = jnp.minimum(code // 8, half - 1), code % 8
-                for f in range(5):
-                    pick[5 + f, s : s + 1, :] = known[q, 5 + f, pl.ds(sigma, 1), :]
-                    pick[5 + f, 8 + s : 9 + s, :] = known[q, 5 + f, pl.ds(8 + sigma, 1), :]
-            shifts = []
-            for s in range(OUT):
-                code = entry(first_kind + 1, 1, s)
-                q, sigma = jnp.minimum(code // 8, half - 1), code % 8
-                shifts.append((q, lax.rem(edge * (s + 8 - sigma), LANES)))
-            for f in range(5):
-                tile = None
-                for s, (q, shift) in enumerate(shifts):
-                    piece = pltpu.roll(known[q, f], shift, 1)
-                    tile = piece if tile is None else jnp.where(tile_lane // edge == s, piece, tile)
-                pick[f] = tile
-
-        for level in range(levels - 1):
-            size = 1 << level
-            for known, flights in ((lo_known, flights_lo), (hi_known, flights_hi)):
-                flights[-1].wait()
-                flights.append(
-                    remote(known.at[pl.ds(0, size)], known.at[pl.ds(size, size)], partner(level))
-                )
-        for known, flights, pick, sel, kind in (
-            (lo_known, flights_lo, lo_pick, lo_sel, 0),
-            (hi_known, flights_hi, hi_pick, hi_sel, 2),
-        ):
-            flights[-1].wait()
-            select(known, pick, kind)
-            flights.append(remote(pick, sel, partner(levels - 1)))
-        flights_lo[-1].wait()
-        flights_hi[-1].wait()
-
-        def advance(slot, carry):
+    def advance(step, n):
+        lo_known, hi_known, _, _, lo_sel, hi_sel = sections[step][2:]
+
+        def run(slot, carry):
             def place(kind):
-                code = entry(kind, 0, slot)
-                near = code < 8 * half
-                q = jnp.minimum(code // 8, half - 1)
-                return near, q, jnp.where(near, code % 8, slot)
-
-            def x_row(known, sel, seat, f, top):
+                code = entry(step, kind, 0, slot)
+                return code < 16 * half, *near_seat(code)
+
+            def x_row(known, sel, seat, f):
                 near, q, sigma = seat
-                a = known[q, 5 + f, pl.ds(top + sigma, 1), :]
-                b = sel[5 + f, pl.ds(top + slot, 1), :]
-                return jnp.where(near, a, b)
+                parts = []
+                for part in range(2):
+                    unit, row = x_seat(n, sigma, f, part)
+                    unit2, row2 = x_seat(OUT, slot, f, part)
+                    a = known[q, unit, pl.ds(row, 1), :]
+                    b = sel[unit2, pl.ds(row2, 1), :]
+                    parts.append(jnp.where(near, a, b))
+                return jnp.concatenate(parts, axis=1)
 
             def y_tile(known, sel, seat, f, to):
                 near, q, sigma = seat
-                tile = jnp.where(near, known[q, f], sel[f])
-                return pltpu.roll(tile, lax.rem(LANES + to - edge * sigma, LANES), 1)
+                unit, lane = y_seat(sigma, f)
+                unit2, lane2 = y_seat(slot, f)
+                tile = jnp.where(near, tile_of(known, q, unit), tile_of(sel, unit2))
+                lane = jnp.where(near, lane, lane2)
+                return pltpu.roll(tile, lax.rem(LANES + to - lane, LANES), 1)
 
             x_lo, y_lo, x_hi, y_hi = (place(kind) for kind in range(4))
             ghost_x, ghost_y = [], []
             for f in range(5):
-                low = jnp.concatenate(
-                    [x_row(lo_known, lo_sel, x_lo, f, 0), x_row(lo_known, lo_sel, x_lo, f, 8)], axis=1
-                )
-                high = jnp.concatenate(
-                    [x_row(hi_known, hi_sel, x_hi, f, 0), x_row(hi_known, hi_sel, x_hi, f, 8)], axis=1
-                )
+                low = x_row(lo_known, lo_sel, x_lo, f)
+                high = x_row(hi_known, hi_sel, x_hi, f)
                 ghost_x.append(jnp.where(ghost_row == 0, low, high))
-                ghost_y.append(
-                    jnp.where(
-                        tile_lane < edge,
-                        y_tile(lo_known, lo_sel, y_lo, f, 0),
-                        y_tile(hi_known, hi_sel, y_hi, f, LANES - edge),
-                    )
-                )
+                low = y_tile(lo_known, lo_sel, y_lo, f, 0)
+                high = y_tile(hi_known, hi_sel, y_hi, f, LANES - edge)
+                ghost_y.append(jnp.where(tile_lane < edge, low, high))
+            if step == 0:
+                ghost_x, ghost_y = conserved(ghost_x), conserved(ghost_y)
             cons = tuple(now[slot, f] for f in range(5))
             rate = block_rate(cons, tuple(ghost_x), tuple(ghost_y))
             moved = [c + DT * d for c, d in zip(cons, rate)]
@@ -339,7 +378,23 @@
                     now[slot, f] = moved[f]
             return carry
 
-        lax.fori_loop(0, OUT, advance, 0)
+        lax.fori_loop(0, OUT, run, 0)
+
+    moving = move_blocks(0)
+    flights = begin(0, cells, cap)
+    flights = gather(0, flights)
+    for level in range(1, levels):
+        moving.wait()
+        moving = move_blocks(level)
+    flights = trade(0, cap, flights)
+    moving.wait()
+    lax.fori_loop(0, OUT, open_block, 0)
+    for step in range(3):
+        if step:
+            flights = trade(step, OUT, gather(step, begin(step, now, OUT)))
+        for flight in flights:
+            flight.wait()
+        advance(step, OUT if step else cap)
 
 
 def body(rows, cols, block_cells, slot_blocks):
@@ -349,13 +404,14 @@
     edge, flat = block_cells.shape[2:]
     table = make_tables(slot_blocks, rows, cols, lax.axis_index("row"), lax.axis_index("col"))
     block = (5, edge, flat)
-    faces = (10, 16, LANES)
     scratch = [pltpu.VMEM((SEND, *block), jnp.float32) for _ in range(2 * levels)]
     scratch += [pltpu.VMEM((OUT, *block), jnp.float32) for _ in range(2)]
-    for _ in range(3):
+    for step in range(3):
+        faces = (units(OUT if step else cap), 8, LANES)
+        picked = (units(OUT), 8, LANES)
         scratch += [pltpu.VMEM(faces, jnp.float32) for _ in range(2)]
         scratch += [pltpu.VMEM((half, *faces), jnp.float32) for _ in range(2)]
-        scratch += [pltpu.VMEM(faces, jnp.float32) for _ in range(4)]
+        scratch += [pltpu.VMEM(picked, jnp.float32) for _ in range(4)]
     scratch += [pltpu.SemaphoreType.DMA((levels,)) for _ in range(2)]
     scratch += [pltpu.SemaphoreType.DMA((3, 2 * (levels + 1))) for _ in range(2)]
     return pl.pallas_call(

time: 93.9 us -> 90.1 us (0.960)
  Pallas kernels: 85.7 us -> 81.7 us
  local copies, waits for them, and re-layouts: 4.17 us -> 6.25 us
  other arithmetic: 3.68 us -> 1.81 us
    pallas_call x1, Pallas kernels: 85.7 us -> 81.7 us  [body(): pl.pallas_call(functools.partial(kernel, rows, cols, cap), out_shape=jax....]
    concatenate x0 -> x1, local copies, waits for them, and re-layouts: none -> 1.97 us  [make_tables(): return jnp.concatenate([jnp.stack(scalars), source])]
    concatenate x1 -> x0, other arithmetic: 1.96 us -> none  [make_tables(): return jnp.concatenate([jnp.stack(scalars), source])]
where the time goes in v2:
time: 90.1 us; the launch traced here: 89.9 us
  Pallas kernels  81.7 us (91%)
  local copies, waits for them, and re-layouts  6.25 us (7%)
  other arithmetic  1.81 us (2%)
    pallas_call x1, Pallas kernels, body(): pl.pallas_call(functools.partial(kernel, rows, cols, cap), out_shape=jax....  81.7 us
    unnamed x6, local copies, waits for them, and re-layouts  2.7 us
    concatenate x1, local copies, waits for them, and re-layouts, make_tables(): return jnp.concatenate([jnp.stack(scalars), source])  1.97 us

profile of v2, /device:TPU:0, one launch (start us, length us, event | category | flops | bytes accessed | tf_op | source)
XLA Modules:
  0.0 89.9 jit_solution(8501598593094382070)
XLA Ops:
  0.0 0.1 add_multiply_fusion
  0.1 0.6 copy-done.1
  0.7 0.1 iota_add_fusion.1
  0.8 0.1 add.312
  0.9 0.1 iota_add_fusion
  1.0 0.1 reduce_sum.105
  1.1 0.1 reshape.512
  1.2 0.1 reduce_sum.103
  1.3 0.8 fusion.2
  2.1 0.1 eq.114
  2.2 0.1 select_reduce_fusion.3
  2.3 0.1 reduce_sum.111
  2.4 0.1 reshape.516
  2.5 0.1 select_reduce_fusion.4
  2.6 0.1 reduce_sum.109
  2.7 0.1 iota_select_fusion
  2.8 0.1 select_reduce_fusion.1
  2.8 0.1 reduce_sum.115
  2.9 0.1 reduce_sum.113
  3.1 0.1 broadcast_in_dim.123
  3.1 0.1 broadcast_in_dim.126
  3.2 0.1 copy.4
  3.3 0.1 eq.102
  3.4 0.1 broadcast_in_dim.128
  3.6 0.1 broadcast_in_dim.118
  3.7 0.2 select_reduce_fusion.5
  3.9 0.1 eq.115
  4.0 0.2 select_reduce_fusion
  4.2 2.0 %concatenate.7.refs_0_ = s32[115]{0:T(128)S(1)} concatenate(s32[1]{0:T(128)} %bitcast.1, s32[1]{0:T(128)} %bitcast.4, s32[1]{0:T(128)} %bitcast.5, s32[56]{0:T(128)S(1)} %and_select_fusion.6, s32[56]{0:T(128)S(1)} %get-tuple-element.10), dimensions={0} | concatenate | bytes 920 | tf_op jit(solution)/shard_map/concatenate | solution.py:70
  6.2 1.2 %copy-done = f32[11,5,16,256]{3,2,1,0:T(8,128)S(1)} copy-done((f32[11,5,16,256]{3,2,1,0:T(8,128)S(1)}, f32[11,5,16,256]{3,2,1,0:T(8,128)}, u32[]{:S(2)}) %copy-start) | copy-done | bytes 901144
  7.4 81.7 %shard_map.28 = f32[7,5,16,256]{3,2,1,0:T(8,128)S(1)} custom-call(s32[115]{0:T(128)S(1)} %concatenate.7.refs_0_, f32[11,5,16,256]{3,2,1,0:T(8,128)S(1)} %copy-done), custom_call_target="tpu_custom_call" | custom-call | tf_op jit(solution)/shard_map/pallas_call | solution.py:417
  89.0 0.8 copy.6
  (20 shorter events, 0.2 us)
Async XLA Ops:
  0.0 0.7 copy-start.1
  6.2 1.2 %copy-start = (f32[11,5,16,256]{3,2,1,0:T(8,128)S(1)}, f32[11,5,16,256]{3,2,1,0:T(8,128)}, u32[]{:S(2)}) copy-start(f32[11,5,16,256]{3,2,1,0:T(8,128)} %refs_1_.1) | copy-start | bytes 2703364

commit v3 on v2

--- a/solution.py
+++ b/solution.py
@@ -136,7 +136,7 @@
     mid = direction_values(cons, values, 2)
     up = [pltpu.roll(m, flat - 1, 1) for m in mid]
     upper = face(mid, up)
-    height = lane % edge
+    height = lane & (edge - 1)
     zero = jnp.zeros_like(values[1])
     wall = [zero, zero, zero, values[1], zero]
     change = [
@@ -160,12 +160,12 @@
 
 def y_seat(slot, f):
     at = slot * 5 + f
-    return 2 * (at // 8), 16 * (at % 8)
+    return 2 * (at >> 3), 16 * (at & 7)
 
 
 def x_seat(n, slot, f, part):
     at = slot * 10 + 2 * f + part
-    return y_units(n) + at // 8, at % 8
+    return y_units(n) + (at >> 3), at & 7
 
 
 def kernel(rows, cols, cap, *refs):
@@ -203,6 +203,7 @@
 
     edge, flat = now.shape[2:]
     tile_lane = lax.broadcasted_iota(jnp.int32, (edge, LANES), 1)
+    tile_group = tile_lane >> 4
     ghost_row = lax.broadcasted_iota(jnp.int32, (8, 2 * LANES), 0)
 
     def tile_of(ref, *seat):
@@ -248,7 +249,7 @@
                 shift = (edge * (at - first) + (edge if high else 0)) % LANES
                 piece = blocks[s, f, :, side]
                 piece = pltpu.roll(piece, shift, 1) if shift else piece
-                tile = piece if tile is None else jnp.where(tile_lane // edge == at - first, piece, tile)
+                tile = piece if tile is None else jnp.where(tile_group == at - first, piece, tile)
             put_tile(buffer, 2 * (first // 8), tile)
         for s in range(n):
             for f in range(5):
@@ -264,7 +265,7 @@
         return tab[base + ((8 * OUT if step else 0) + (kind * 2 + far) * OUT + slot)]
 
     def near_seat(code):
-        return jnp.minimum(code // 16, half - 1), code % 16
+        return jnp.minimum(code >> 4, half - 1), code & 15
 
     def select(step, n, known, pick, first_kind):
         for s in range(OUT):
@@ -280,9 +281,9 @@
             for at in range(first, min(first + 8, 5 * OUT)):
                 q, sigma = seats[at // 5]
                 unit, lane = y_seat(sigma, at % 5)
-                shift = lax.rem(edge * (at - first) + LANES - lane, LANES)
+                shift = (edge * (at - first) + LANES - lane) & (LANES - 1)
                 piece = pltpu.roll(tile_of(known, q, unit), shift, 1)
-                tile = piece if tile is None else jnp.where(tile_lane // edge == at - first, piece, tile)
+                tile = piece if tile is None else jnp.where(tile_group == at - first, piece, tile)
             put_tile(pick, 2 * (first // 8), tile)
 
     def begin(step, blocks, n):
@@ -345,7 +346,7 @@
                 unit2, lane2 = y_seat(slot, f)
                 tile = jnp.where(near, tile_of(known, q, unit), tile_of(sel, unit2))
                 lane = jnp.where(near, lane, lane2)
-                return pltpu.roll(tile, lax.rem(LANES + to - lane, LANES), 1)
+                return pltpu.roll(tile, (LANES + to - lane) & (LANES - 1), 1)
 
             x_lo, y_lo, x_hi, y_hi = (place(kind) for kind in range(4))
             ghost_x, ghost_y = [], []

time: 90.1 us -> 85.7 us (0.951)
  Pallas kernels: 81.7 us -> 77.3 us
    pallas_call x1, Pallas kernels: 81.7 us -> 77.3 us  [body(): pl.pallas_call(functools.partial(kernel, rows, cols, cap), out_shape=jax....]
where the time goes in v3:
time: 85.7 us; the launch traced here: 85.5 us
  Pallas kernels  77.3 us (90%)
  local copies, waits for them, and re-layouts  6.25 us (7%)
  other arithmetic  1.81 us (2%)
    pallas_call x1, Pallas kernels, body(): pl.pallas_call(functools.partial(kernel, rows, cols, cap), out_shape=jax....  77.3 us
    unnamed x6, local copies, waits for them, and re-layouts  2.7 us
    concatenate x1, local copies, waits for them, and re-layouts, make_tables(): return jnp.concatenate([jnp.stack(scalars), source])  1.97 us

profile of v3, /device:TPU:0, one launch (start us, length us, event | category | flops | bytes accessed | tf_op | source)
XLA Modules:
  0.0 85.5 jit_solution(153680088754545310)
XLA Ops:
  0.0 0.1 add_multiply_fusion
  0.1 0.6 copy-done.1
  0.7 0.1 iota_add_fusion.1
  0.8 0.1 add.312
  0.9 0.1 iota_add_fusion
  1.0 0.1 reduce_sum.105
  1.1 0.1 reshape.512
  1.2 0.1 reduce_sum.103
  1.3 0.8 fusion.2
  2.1 0.1 eq.114
  2.2 0.1 select_reduce_fusion.3
  2.3 0.1 reduce_sum.111
  2.4 0.1 reshape.516
  2.5 0.1 select_reduce_fusion.4
  2.6 0.1 reduce_sum.109
  2.7 0.1 iota_select_fusion
  2.8 0.1 select_reduce_fusion.1
  2.8 0.1 reduce_sum.115
  2.9 0.1 reduce_sum.113
  3.1 0.1 broadcast_in_dim.123
  3.1 0.1 broadcast_in_dim.126
  3.2 0.1 copy.4
  3.3 0.1 eq.102
  3.4 0.1 broadcast_in_dim.128
  3.6 0.1 broadcast_in_dim.118
  3.7 0.2 select_reduce_fusion.5
  3.9 0.1 eq.115
  4.0 0.2 select_reduce_fusion
  4.2 2.0 %concatenate.7.refs_0_ = s32[115]{0:T(128)S(1)} concatenate(s32[1]{0:T(128)} %bitcast.1, s32[1]{0:T(128)} %bitcast.4, s32[1]{0:T(128)} %bitcast.5, s32[56]{0:T(128)S(1)} %and_select_fusion.6, s32[56]{0:T(128)S(1)} %get-tuple-element.10), dimensions={0} | concatenate | bytes 920 | tf_op jit(solution)/shard_map/concatenate | solution.py:70
  6.2 1.2 %copy-done = f32[11,5,16,256]{3,2,1,0:T(8,128)S(1)} copy-done((f32[11,5,16,256]{3,2,1,0:T(8,128)S(1)}, f32[11,5,16,256]{3,2,1,0:T(8,128)}, u32[]{:S(2)}) %copy-start) | copy-done | bytes 901144
  7.4 77.3 %shard_map.28 = f32[7,5,16,256]{3,2,1,0:T(8,128)S(1)} custom-call(s32[115]{0:T(128)S(1)} %concatenate.7.refs_0_, f32[11,5,16,256]{3,2,1,0:T(8,128)S(1)} %copy-done), custom_call_target="tpu_custom_call" | custom-call | tf_op jit(solution)/shard_map/pallas_call | solution.py:418
  84.7 0.8 copy.6
  (20 shorter events, 0.2 us)
Async XLA Ops:
  0.0 0.7 copy-start.1
  6.2 1.2 %copy-start = (f32[11,5,16,256]{3,2,1,0:T(8,128)S(1)}, f32[11,5,16,256]{3,2,1,0:T(8,128)}, u32[]{:S(2)}) copy-start(f32[11,5,16,256]{3,2,1,0:T(8,128)} %refs_1_.1) | copy-start | bytes 2703364

commit v4 on v3

--- a/solution.py
+++ b/solution.py
@@ -49,24 +49,25 @@
     flat_ids = ids.reshape(-1)
     flat_place = jnp.where(flat_ids >= 0, place.reshape(-1), 0)
     flat_col = jnp.broadcast_to(col_ids[None, :, None], ids.shape).reshape(-1)
-    seats = jnp.stack([my_row, my_row ^ half])[:, None] * 16 + jnp.arange(OUT, dtype=jnp.int32)
-    seats = seats.reshape(-1)
-    match = (flat_place[None] == seats[:, None]) & (flat_col == my_col)[None] & (flat_ids >= 0)[None]
-    along = jnp.sum(jnp.where(match, flat_ids[None] - my_col * group, 0), axis=1)
-    below = ((my_col + cols - 1) % cols) * group
-    above = ((my_col + 1) % cols) * group
-    wanted = jnp.stack(
-        [
-            below + along,
-            below + (along + group - 1) % group,
-            above + along,
-            above + (along + 1) % group,
-        ]
-    ).reshape(-1)
+    near_far = jnp.stack([my_row, my_row ^ half])
+    left, right = (my_col + cols - 1) % cols, (my_col + 1) % cols
+    seat_rows = jnp.concatenate([near_far[:1], near_far, near_far])
+    seat_cols = jnp.stack([my_col, right, right, left, left])
+    seats = (seat_rows[:, None] * 16 + jnp.arange(OUT, dtype=jnp.int32)).reshape(-1, 1)
+    seat_cols = jnp.repeat(seat_cols, OUT)[:, None]
+    match = (flat_place[None] == seats) & (flat_col[None] == seat_cols) & (flat_ids >= 0)[None]
+    along = jnp.sum(jnp.where(match, flat_ids[None] - flat_col[None] * group, 0), axis=1)
+    along = along.reshape(5, OUT)
+    here, there_right, there_left = along[:1], along[1:3], along[3:5]
+    down, up = (lambda a: (a + group - 1) % group), (lambda a: (a + 1) % group)
+    mine = jnp.concatenate([left * group + here, left * group + down(here)])
+    mine = jnp.concatenate([mine, right * group + here, right * group + up(here)])
+    theirs = jnp.concatenate([there_right, down(there_right), there_left, up(there_left)])
+    wanted = jnp.concatenate([mine, theirs + my_col * group]).reshape(-1)
     both = flat_place * 4096 + origin
     found = jnp.sum(jnp.where(flat_ids[None] == wanted[:, None], both[None], 0), axis=1)
     source = found ^ (my_row * 16 * 4097)
-    source = jnp.concatenate([source % 4096, source // 4096])
+    source = jnp.concatenate([source & 4095, source >> 12])
     return jnp.concatenate([jnp.stack(scalars), source])
 
 
@@ -178,8 +179,8 @@
     recv_blocks = refs[levels : 2 * levels]
     refs = refs[2 * levels :]
     start, now = refs[:2]
-    sections = [refs[2 + 8 * i : 10 + 8 * i] for i in range(3)]
-    bsend, brecv, hsend, hrecv = refs[26:30]
+    sections = [refs[2 + 10 * i : 12 + 10 * i] for i in range(3)]
+    bsend, brecv, hsend, hrecv = refs[32:36]
     my_row, my_col = lax.axis_index("row"), lax.axis_index("col")
     left = (my_row, lax.rem(my_col + cols - 1, cols))
     right = (my_row, lax.rem(my_col + 1, cols))
@@ -189,9 +190,11 @@
         return (my_row + bit - 2 * bit * (lax.rem(my_row // bit, 2)), my_col)
 
     barrier = pltpu.get_barrier_semaphore()
-    for device in [left, right] + [partner(level) for level in range(levels)]:
+    across = partner(levels - 1)[0]
+    beside = [(right, left), ((across, right[1]), (across, left[1]))]
+    for device in [*beside[0], *beside[1]] + [partner(level) for level in range(levels)]:
         pl.semaphore_signal(barrier, inc=1, device_id=device, device_id_type=MESH)
-    pl.semaphore_wait(barrier, 2 + levels)
+    pl.semaphore_wait(barrier, 4 + levels)
 
     def held(slot, depth):
         value = cells[jnp.minimum(slot, cap - 1)]
@@ -262,20 +265,21 @@
     base = levels + 1
 
     def entry(step, kind, far, slot):
-        return tab[base + ((8 * OUT if step else 0) + (kind * 2 + far) * OUT + slot)]
+        at = kind * OUT if far is None else 4 * OUT + (kind * 2 + far) * OUT
+        return tab[base + (12 * OUT if step else 0) + at + slot]
 
     def near_seat(code):
         return jnp.minimum(code >> 4, half - 1), code & 15
 
-    def select(step, n, known, pick, first_kind):
+    def select(step, n, known, pick, first_kind, far):
         for s in range(OUT):
-            q, sigma = near_seat(entry(step, first_kind, 1, s))
+            q, sigma = near_seat(entry(step, first_kind, far, s))
             for f in range(5):
                 for part in range(2):
                     unit, row = x_seat(n, sigma, f, part)
                     to, at = x_seat(OUT, s, f, part)
                     pick[to, at : at + 1, :] = known[q, unit, pl.ds(row, 1), :]
-        seats = [near_seat(entry(step, first_kind + 1, 1, s)) for s in range(OUT)]
+        seats = [near_seat(entry(step, first_kind + 1, far, s)) for s in range(OUT)]
         for first in range(0, 5 * OUT, 8):
             tile = None
             for at in range(first, min(first + 8, 5 * OUT)):
@@ -287,32 +291,40 @@
             put_tile(pick, 2 * (first // 8), tile)
 
     def begin(step, blocks, n):
-        hi_send, lo_send, lo_known, hi_known = sections[step][:4]
-        pack(blocks, n, hi_send, True)
-        low = remote(step, 0, hi_send, lo_known.at[0], right)
-        pack(blocks, n, lo_send, False)
-        return [low, remote(step, 1, lo_send, hi_known.at[0], left)]
+        flights = []
+        for side in range(2):
+            known = sections[step][side]
+            pack(blocks, n, known.at[0], side == 0)
+            if levels > 1:
+                flights.append(remote(step, side, known.at[0], known.at[1], partner(0)))
+        return flights
 
     def gather(step, flights):
-        at = 2
-        for level in range(levels - 1):
+        for level in range(1, levels - 1):
             size = 1 << level
             for side in range(2):
-                known = sections[step][2 + side]
+                known = sections[step][side]
                 flights[side].wait()
                 flights[side] = remote(
-                    step, at, known.at[pl.ds(0, size)], known.at[pl.ds(size, size)], partner(level)
+                    step,
+                    2 * level + side,
+                    known.at[pl.ds(0, size)],
+                    known.at[pl.ds(size, size)],
+                    partner(level),
                 )
-                at += 1
         return flights
 
     def trade(step, n, flights):
+        sent = []
         for side in range(2):
-            known, pick, sel = (sections[step][at + side] for at in (2, 4, 6))
-            flights[side].wait()
-            select(step, n, known, pick, 2 * side)
-            flights[side] = remote(step, 2 * levels + side, pick, sel, partner(levels - 1))
-        return flights
+            if flights:
+                flights[side].wait()
+            for far in (1, 0):
+                known, pick, sel = (sections[step][at] for at in (side, 2 + 2 * side + far, 6 + 2 * side + far))
+                select(step, n, known, pick, 2 * side, far)
+                at = 2 * (levels - 1) + 2 * side + far
+                sent.append(remote(step, at, pick, sel, beside[far][side]))
+        return sent
 
     def open_block(slot, carry):
         value = held(slot, levels)
@@ -321,41 +333,34 @@
             now[slot, f] = field
         return carry
 
-    def advance(step, n):
-        lo_known, hi_known, _, _, lo_sel, hi_sel = sections[step][2:]
+    def advance(step):
+        lo_near, lo_far, hi_near, hi_far = sections[step][6:]
 
         def run(slot, carry):
-            def place(kind):
-                code = entry(step, kind, 0, slot)
-                return code < 16 * half, *near_seat(code)
-
-            def x_row(known, sel, seat, f):
-                near, q, sigma = seat
+            def near(kind):
+                return entry(step, kind, None, slot) < 16 * half
+
+            def x_row(close, away, kind, f):
                 parts = []
                 for part in range(2):
-                    unit, row = x_seat(n, sigma, f, part)
-                    unit2, row2 = x_seat(OUT, slot, f, part)
-                    a = known[q, unit, pl.ds(row, 1), :]
-                    b = sel[unit2, pl.ds(row2, 1), :]
-                    parts.append(jnp.where(near, a, b))
+                    unit, row = x_seat(OUT, slot, f, part)
+                    a = close[unit, pl.ds(row, 1), :]
+                    b = away[unit, pl.ds(row, 1), :]
+                    parts.append(jnp.where(near(kind), a, b))
                 return jnp.concatenate(parts, axis=1)
 
-            def y_tile(known, sel, seat, f, to):
-                near, q, sigma = seat
-                unit, lane = y_seat(sigma, f)
-                unit2, lane2 = y_seat(slot, f)
-                tile = jnp.where(near, tile_of(known, q, unit), tile_of(sel, unit2))
-                lane = jnp.where(near, lane, lane2)
+            def y_tile(close, away, kind, f, to):
+                unit, lane = y_seat(slot, f)
+                tile = jnp.where(near(kind), tile_of(close, unit), tile_of(away, unit))
                 return pltpu.roll(tile, (LANES + to - lane) & (LANES - 1), 1)
 
-            x_lo, y_lo, x_hi, y_hi = (place(kind) for kind in range(4))
             ghost_x, ghost_y = [], []
             for f in range(5):
-                low = x_row(lo_known, lo_sel, x_lo, f)
-                high = x_row(hi_known, hi_sel, x_hi, f)
+                low = x_row(lo_near, lo_far, 0, f)
+                high = x_row(hi_near, hi_far, 2, f)
                 ghost_x.append(jnp.where(ghost_row == 0, low, high))
-                low = y_tile(lo_known, lo_sel, y_lo, f, 0)
-                high = y_tile(hi_known, hi_sel, y_hi, f, LANES - edge)
+                low = y_tile(lo_near, lo_far, 1, f, 0)
+                high = y_tile(hi_near, hi_far, 3, f, LANES - edge)
                 ghost_y.append(jnp.where(tile_lane < edge, low, high))
             if step == 0:
                 ghost_x, ghost_y = conserved(ghost_x), conserved(ghost_y)
@@ -395,7 +400,7 @@
             flights = trade(step, OUT, gather(step, begin(step, now, OUT)))
         for flight in flights:
             flight.wait()
-        advance(step, OUT if step else cap)
+        advance(step)
 
 
 def body(rows, cols, block_cells, slot_blocks):
@@ -410,9 +415,8 @@
     for step in range(3):
         faces = (units(OUT if step else cap), 8, LANES)
         picked = (units(OUT), 8, LANES)
-        scratch += [pltpu.VMEM(faces, jnp.float32) for _ in range(2)]
         scratch += [pltpu.VMEM((half, *faces), jnp.float32) for _ in range(2)]
-        scratch += [pltpu.VMEM(picked, jnp.float32) for _ in range(4)]
+        scratch += [pltpu.VMEM(picked, jnp.float32) for _ in range(8)]
     scratch += [pltpu.SemaphoreType.DMA((levels,)) for _ in range(2)]
     scratch += [pltpu.SemaphoreType.DMA((3, 2 * (levels + 1))) for _ in range(2)]
     return pl.pallas_call(

time: 85.7 us -> 83.6 us (0.975)
  Pallas kernels: 77.3 us -> 74.7 us
    pallas_call x1, Pallas kernels: 77.3 us -> 74.7 us  [body(): pl.pallas_call(functools.partial(kernel, rows, cols, cap), out_shape=jax....]
where the time goes in v4:
time: 83.6 us; the launch traced here: 83.3 us
  Pallas kernels  74.7 us (89%)
  local copies, waits for them, and re-layouts  6.79 us (8%)
  other arithmetic  1.74 us (2%)
    pallas_call x1, Pallas kernels, body(): pl.pallas_call(functools.partial(kernel, rows, cols, cap), out_shape=jax....  74.7 us
    unnamed x6, local copies, waits for them, and re-layouts  2.6 us
    concatenate x1, local copies, waits for them, and re-layouts, make_tables(): return jnp.concatenate([jnp.stack(scalars), source])  1.97 us

profile of v4, /device:TPU:0, one launch (start us, length us, event | category | flops | bytes accessed | tf_op | source)
XLA Modules:
  0.0 83.3 jit_solution(1089992624742058911)
XLA Ops:
  0.0 0.1 concatenate.23
  0.1 0.1 stack.32
  0.2 0.5 copy-done.1
  0.8 0.1 reduce_sum.105
  0.9 0.1 reshape.495
  1.1 0.1 reduce_sum.103
  1.1 0.8 fusion.2
  2.0 0.1 eq.121
  2.2 0.1 add.276
  2.3 0.1 reduce_sum.111
  2.4 0.1 reshape.499
  2.6 0.1 reduce_sum.109
  2.7 0.1 iota_select_fusion
  2.8 0.1 select_reduce_fusion.1
  2.9 0.1 reduce_sum.115
  3.0 0.1 reduce_sum.113
  3.2 0.1 broadcast_in_dim.130
  3.3 0.1 copy.4
  3.4 0.1 eq.109
  3.5 0.1 eq.119
  3.6 0.1 broadcast_in_dim.132
  3.7 0.1 broadcast_in_dim.122
  3.8 0.2 select_reduce_fusion.5
  4.1 0.1 slice.34
  4.2 0.1 slice.36
  4.3 0.1 concatenate.25
  4.4 0.1 eq.124
  4.5 0.2 select_reduce_fusion
  4.7 2.0 %concatenate.26.refs_0_ = s32[171]{0:T(256)S(1)} concatenate(s32[1]{0:T(128)} %bitcast.1, s32[1]{0:T(128)} %bitcast.4, s32[1]{0:T(128)} %bitcast.5, s32[84]{0:T(128)S(1)} %get-tuple-element.17, s32[84]{0:T(128)S(1)} %get-tuple-element.16), dimensions={0} | concatenate | bytes 1368 | tf_op jit(solution)/shard_map/concatenate | solution.py:71
  6.7 1.2 %copy-done = f32[11,5,16,256]{3,2,1,0:T(8,128)S(1)} copy-done((f32[11,5,16,256]{3,2,1,0:T(8,128)S(1)}, f32[11,5,16,256]{3,2,1,0:T(8,128)}, u32[]{:S(2)}) %copy-start) | copy-done | bytes 901144
  7.9 74.7 %shard_map.28 = f32[7,5,16,256]{3,2,1,0:T(8,128)S(1)} custom-call(s32[171]{0:T(256)S(1)} %concatenate.26.refs_0_, f32[11,5,16,256]{3,2,1,0:T(8,128)S(1)} %copy-done), custom_call_target="tpu_custom_call" | custom-call | tf_op jit(solution)/shard_map/pallas_call | solution.py:422
  82.5 0.8 copy.6
  (27 shorter events, 0.7 us)
Async XLA Ops:
  0.0 0.7 copy-start.1
  6.7 1.2 %copy-start = (f32[11,5,16,256]{3,2,1,0:T(8,128)S(1)}, f32[11,5,16,256]{3,2,1,0:T(8,128)}, u32[]{:S(2)}) copy-start(f32[11,5,16,256]{3,2,1,0:T(8,128)} %refs_1_.1) | copy-start | bytes 2703364

commit v5 on v4

--- a/solution.py
+++ b/solution.py
@@ -316,10 +316,10 @@
 
     def trade(step, n, flights):
         sent = []
-        for side in range(2):
-            if flights:
-                flights[side].wait()
-            for far in (1, 0):
+        for far in (1, 0):
+            for side in range(2):
+                if flights and far:
+                    flights[side].wait()
                 known, pick, sel = (sections[step][at] for at in (side, 2 + 2 * side + far, 6 + 2 * side + far))
                 select(step, n, known, pick, 2 * side, far)
                 at = 2 * (levels - 1) + 2 * side + far

time: 83.6 us -> 84 us (level)
  no operation moved by 1% of the time
where the time goes in v5:
time: 84 us; the launch traced here: 83.8 us
  Pallas kernels  75.1 us (89%)
  local copies, waits for them, and re-layouts  6.79 us (8%)
  other arithmetic  1.74 us (2%)
    pallas_call x1, Pallas kernels, body(): pl.pallas_call(functools.partial(kernel, rows, cols, cap), out_shape=jax....  75.1 us
    unnamed x6, local copies, waits for them, and re-layouts  2.6 us
    concatenate x1, local copies, waits for them, and re-layouts, make_tables(): return jnp.concatenate([jnp.stack(scalars), source])  1.97 us

profile of v5, /device:TPU:0, one launch (start us, length us, event | category | flops | bytes accessed | tf_op | source)
XLA Modules:
  0.0 83.8 jit_solution(5709944024609502367)
XLA Ops:
  0.0 0.1 concatenate.23
  0.1 0.1 stack.32
  0.2 0.5 copy-done.1
  0.8 0.1 reduce_sum.105
  0.9 0.1 reshape.495
  1.1 0.1 reduce_sum.103
  1.1 0.8 fusion.2
  2.0 0.1 eq.121
  2.2 0.1 add.276
  2.3 0.1 reduce_sum.111
  2.4 0.1 reshape.499
  2.6 0.1 reduce_sum.109
  2.7 0.1 iota_select_fusion
  2.8 0.1 select_reduce_fusion.1
  2.9 0.1 reduce_sum.115
  3.0 0.1 reduce_sum.113
  3.2 0.1 broadcast_in_dim.130
  3.3 0.1 copy.4
  3.4 0.1 eq.109
  3.5 0.1 eq.119
  3.6 0.1 broadcast_in_dim.132
  3.7 0.1 broadcast_in_dim.122
  3.8 0.2 select_reduce_fusion.5
  4.1 0.1 slice.34
  4.2 0.1 slice.36
  4.3 0.1 concatenate.25
  4.4 0.1 eq.124
  4.5 0.2 select_reduce_fusion
  4.7 2.0 %concatenate.26.refs_0_ = s32[171]{0:T(256)S(1)} concatenate(s32[1]{0:T(128)} %bitcast.1, s32[1]{0:T(128)} %bitcast.4, s32[1]{0:T(128)} %bitcast.5, s32[84]{0:T(128)S(1)} %get-tuple-element.17, s32[84]{0:T(128)S(1)} %get-tuple-element.16), dimensions={0} | concatenate | bytes 1368 | tf_op jit(solution)/shard_map/concatenate | solution.py:71
  6.7 1.2 %copy-done = f32[11,5,16,256]{3,2,1,0:T(8,128)S(1)} copy-done((f32[11,5,16,256]{3,2,1,0:T(8,128)S(1)}, f32[11,5,16,256]{3,2,1,0:T(8,128)}, u32[]{:S(2)}) %copy-start) | copy-done | bytes 901144
  7.9 75.1 %shard_map.28 = f32[7,5,16,256]{3,2,1,0:T(8,128)S(1)} custom-call(s32[171]{0:T(256)S(1)} %concatenate.26.refs_0_, f32[11,5,16,256]{3,2,1,0:T(8,128)S(1)} %copy-done), custom_call_target="tpu_custom_call" | custom-call | tf_op jit(solution)/shard_map/pallas_call | solution.py:422
  83.0 0.8 copy.6
  (27 shorter events, 0.7 us)
Async XLA Ops:
  0.0 0.7 copy-start.1
  6.7 1.2 %copy-start = (f32[11,5,16,256]{3,2,1,0:T(8,128)S(1)}, f32[11,5,16,256]{3,2,1,0:T(8,128)}, u32[]{:S(2)}) copy-start(f32[11,5,16,256]{3,2,1,0:T(8,128)} %refs_1_.1) | copy-start | bytes 2703364
